TPU v7x, 32 devices: a whole 2x2x4 slice. The times are simulated.
32 devices in a mesh: img: 2 (over core), row: 2 (over x), col: 8 (over z, y).
Axes of the slice: x: 2, y: 2, z: 4, core: 2. Of those that a mesh axis runs over, the one named last changes fastest.
Arguments:
- images: bfloat16 [8, 32, 128], P('img', 'row', 'col'), may hold values from -4 to 4
- filters: bfloat16 [64, 9, 9], replicated, may hold values from -0.625 to 0.625
- hidden_bias: float32 [64], replicated, may hold values from -3 to -1
- visible_unit_bias: float32 [], replicated, may hold values from -0.5 to 0.5
- unit_noise: bfloat16 [8, 32, 8192], P('img', 'row', 'col'), may hold values from 0.019897461 to 0.9765625
Outputs:
- recon: bfloat16 [8, 32, 128], P('img', 'row', 'col')
- grad_filters: float32 [64, 9, 9], replicated
- grad_hidden: float32 [64], replicated
- grad_visible: float32 [], replicated
All inputs are finite; a program needn't handle non-finite values.
Results may differ from a plain program's by a relative error of at most 0.0075.
Values may be sent and summed in bfloat16 or wider, within the bound.
A program may use at most 64 MiB of HBM per device.

v0:
```python
import functools

import jax
import jax.numpy as jnp
from jax import lax
from jax.experimental import pallas as pl
from jax.experimental.pallas import tpu as pltpu
from jax.sharding import PartitionSpec as P

LANES = 128
MESH = pl.DeviceIdType.MESH
DIRS = [(dr, dc) for dr in (-1, 0, 1) for dc in (-1, 0, 1) if (dr, dc) != (0, 0)]
f32 = jnp.float32
bf16 = jnp.bfloat16


def slot_of(dr, dc):
    return (dr + 1) * 3 + dc + 1


def pooled(e):
    rows = e.shape[0]
    s = e + pltpu.roll(e, LANES // 2, axis=1)
    s3 = s.reshape(rows // 8, 8, LANES)
    even = lax.broadcasted_iota(jnp.int32, s3.shape, 1) % 2 == 0
    t3 = jnp.where(even, pltpu.roll(s3, 7, axis=1), pltpu.roll(s3, 1, axis=1))
    return 1.0 + s + t3.reshape(rows, LANES)


def kernel(
    geo, img_ref, fil_ref, hb_ref, vb_ref, noise_ref, recon_ref, c_out_ref,
    pf, pack, recv_img, ext, a_ref, fp, tz, w_ref, h_ref, s_ref, u_ref, e_ref, recv_e,
    g_ref, acc_ref, c_ref, recv1, recv2, is_sem, ir_sem, es_sem, er_sem, s1_sem, r1_sem, s2_sem, r2_sem,
):
    ni, th, tw, k, filt, n_img, n_row, n_col = geo
    m = filt // 2
    eh, ew = th + 2 * m, tw + 2 * m
    stride = LANES // ni
    rows = ni * th
    blocks = tw * k // LANES
    kp = a_ref.shape[1]
    img_at, row_at, col_at = lax.axis_index("img"), lax.axis_index("row"), lax.axis_index("col")
    n1, n2 = n_img * n_row, n_col
    me1, me2 = img_at * n_row + row_at, col_at

    def exists(dr, dc):
        ok = True
        if dr:
            ok = (row_at > 0) if dr < 0 else (row_at < n_row - 1)
        if dc:
            ok2 = (col_at > 0) if dc < 0 else (col_at < n_col - 1)
            ok = jnp.logical_and(ok, ok2) if dr else ok2
        return ok

    def neighbour(dr, dc):
        return {"row": row_at + dr, "col": col_at + dc}

    def group1(d):
        other = lax.rem(me1 + d, n1)
        return other, {"img": other // n_row, "row": lax.rem(other, n_row)}

    def group2(d):
        other = lax.rem(me2 + d, n2)
        return other, {"col": other}

    recv_img[...] = jnp.zeros_like(recv_img)
    recv_e[...] = jnp.zeros_like(recv_e)
    barrier = pltpu.get_barrier_semaphore()
    count = jnp.int32(n1 - 1 + n2 - 1)
    for d in DIRS:
        @pl.when(exists(*d))
        def _(d=d):
            pl.semaphore_signal(barrier, inc=1, device_id=neighbour(*d), device_id_type=MESH)
        count = count + exists(*d).astype(jnp.int32)
    for d in range(1, n1):
        pl.semaphore_signal(barrier, inc=1, device_id=group1(d)[1], device_id_type=MESH)
    for d in range(1, n2):
        pl.semaphore_signal(barrier, inc=1, device_id=group2(d)[1], device_id_type=MESH)

    pf[...] = jnp.zeros_like(pf)
    for n in range(ni):
        pf[:, n * stride + m : n * stride + m + tw] = img_ref[n].astype(f32)
    pack[...] = pf[...].astype(bf16)

    top = fp.shape[0] - kp
    q = fil_ref.shape[0]
    fp[...] = jnp.zeros_like(fp)
    fv = fil_ref[...].astype(f32)
    per = LANES // k
    for jp in range(per):
        fp[top + jp : top + jp + q, jp * k : (jp + 1) * k] = fv
    pl.semaphore_wait(barrier, count)

    def exchange(make, start):
        for d in DIRS:
            @pl.when(exists(*d))
            def _(d=d):
                cp = make(*d)
                if start:
                    cp.start()
                else:
                    cp.wait()

    def img_copy(dr, dc, start):
        at = slot_of(-dr, -dc) if start else slot_of(dr, dc)
        return pltpu.make_async_remote_copy(
            src_ref=pack, dst_ref=recv_img.at[at], send_sem=is_sem.at[at], recv_sem=ir_sem.at[at],
            device_id=neighbour(dr, dc), device_id_type=MESH,
        )

    for d in DIRS:
        @pl.when(exists(*d))
        def _(d=d):
            img_copy(*d, True).start()

    for b in range(blocks):
        tz[:, b * LANES : (b + 1) * LANES] = fp[top - per * b : top - per * b + kp, :].astype(bf16)
        w_ref[:, b * LANES : (b + 1) * LANES] = 1.0 / jnp.log(noise_ref[:, b * LANES : (b + 1) * LANES].astype(f32))
    a_ref[...] = jnp.zeros_like(a_ref)

    lane = lax.broadcasted_iota(jnp.int32, (th, LANES), 1) % stride

    def place(a_row):
        for n in range(ni):
            for r in range(filt):
                a_ref[a_row + n * th : a_row + (n + 1) * th, r * ew : (r + 1) * ew] = ext[
                    r : r + th, n * stride : n * stride + ew
                ]

    for d in DIRS:
        @pl.when(exists(*d))
        def _(d=d):
            img_copy(*d, True).wait_send()
            img_copy(*d, False).wait_recv()

    for dr in (-1, 0, 1):
        centre = pf[...] if dr == 0 else recv_img[slot_of(dr, 0)].astype(f32)
        left = pltpu.roll(recv_img[slot_of(dr, -1)].astype(f32), LANES - tw, axis=1)
        right = pltpu.roll(recv_img[slot_of(dr, 1)].astype(f32), tw, axis=1)
        band = jnp.where(lane < m, left, jnp.where(lane < m + tw, centre, jnp.where(lane < ew, right, 0.0)))
        if dr == 0:
            ext[m : m + th, :] = band
        elif dr < 0:
            ext[0:m, :] = band[th - m :, :]
        else:
            ext[m + th :, :] = band[:m, :]
    place(0)

    bias = jnp.concatenate([hb_ref[...]] * per, axis=1)
    a_pos = a_ref[0:rows, :].astype(bf16)
    hidden = jnp.zeros((8, LANES), f32)

    def fold(x):
        return jnp.sum(x.reshape(rows // 8, 8, LANES), axis=0)

    step = 2 * LANES if blocks % 2 == 0 else LANES
    for b0 in range(0, blocks * LANES, step):
        xw = jnp.dot(a_pos, tz[:, b0 : b0 + step], preferred_element_type=f32)
        for o in range(0, step, LANES):
            at = b0 + o
            e = jnp.exp(xw[:, o : o + LANES] + bias)
            prob = e / pooled(e)
            hidden = hidden + fold(prob)
            h_ref[0:rows, at : at + LANES] = prob.astype(bf16)
            t = e * w_ref[:, at : at + LANES]
            t = t * t
            s_ref[:, at : at + LANES] = (t / pooled(t)).astype(bf16)

    u_ref[...] = lax.dot_general(s_ref[...], tz[...], (((1,), (1,)), ((), ())), preferred_element_type=f32)
    e_ref[...] = jnp.zeros_like(e_ref)
    gap = jnp.zeros((th, stride - ew), f32)
    for r in range(filt):
        pieces = []
        for n in range(ni):
            pieces += [u_ref[n * th : (n + 1) * th, r * ew : (r + 1) * ew], gap]
        e_ref[r : r + th, :] += jnp.concatenate(pieces, axis=1)

    def e_copy(dr, dc, start):
        at = slot_of(-dr, -dc) if start else slot_of(dr, dc)
        way = dr if start else -dr
        if way == 0:
            src, dst = e_ref, recv_e.at[at]
        elif way > 0:
            src, dst = e_ref.at[th:eh], recv_e.at[at, 0 : 2 * m]
        else:
            src, dst = e_ref.at[0 : 2 * m], recv_e.at[at, th:eh]
        return pltpu.make_async_remote_copy(
            src_ref=src, dst_ref=dst, send_sem=es_sem.at[at], recv_sem=er_sem.at[at],
            device_id=neighbour(dr, dc), device_id_type=MESH,
        )

    for d in DIRS:
        @pl.when(exists(*d))
        def _(d=d):
            e_copy(*d, True).start()
    for d in DIRS:
        @pl.when(exists(*d))
        def _(d=d):
            e_copy(*d, True).wait_send()
            e_copy(*d, False).wait_recv()

    elane = lax.broadcasted_iota(jnp.int32, (eh, LANES), 1) % stride
    erow = lax.broadcasted_iota(jnp.int32, (eh, LANES), 0)
    total = e_ref[...] + recv_e[slot_of(-1, 0)] + recv_e[slot_of(1, 0)]
    left = recv_e[slot_of(-1, -1)] + recv_e[slot_of(0, -1)] + recv_e[slot_of(1, -1)]
    right = recv_e[slot_of(-1, 1)] + recv_e[slot_of(0, 1)] + recv_e[slot_of(1, 1)]
    total = total + jnp.where(elane < 2 * m, pltpu.roll(left, LANES - tw, axis=1), 0.0)
    total = total + jnp.where(
        jnp.logical_and(elane >= tw, elane < ew), pltpu.roll(right, tw, axis=1), 0.0
    )
    recon = (total + vb_ref[0]).astype(bf16).astype(f32)
    lo_r = jnp.where(row_at == 0, m, 0)
    hi_r = jnp.where(row_at == n_row - 1, m + th, eh)
    lo_c = jnp.where(col_at == 0, m, 0)
    hi_c = jnp.where(col_at == n_col - 1, m + tw, ew)
    inside = (erow >= lo_r) & (erow < hi_r) & (elane >= lo_c) & (elane < hi_c)
    ext[...] = jnp.where(inside, recon, 0.0)
    own = ext[m : m + th, :]
    for n in range(ni):
        recon_ref[n] = own[:, n * stride + m : n * stride + m + tw].astype(bf16)
    mine = jnp.logical_and(lane >= m, lane < m + tw)
    visible = jnp.sum(jnp.where(mine, pf[...] - own, 0.0))
    place(rows)

    a_neg = a_ref[rows : 2 * rows, :].astype(bf16)
    for b0 in range(0, blocks * LANES, step):
        xw = jnp.dot(a_neg, tz[:, b0 : b0 + step], preferred_element_type=f32)
        for o in range(0, step, LANES):
            at = b0 + o
            e = jnp.exp(xw[:, o : o + LANES] + bias)
            prob = e / pooled(e)
            hidden = hidden - fold(prob)
            h_ref[rows : 2 * rows, at : at + LANES] = (-prob).astype(bf16)

    a_all = a_ref[...].astype(bf16)
    q_len = acc_ref.shape[0]
    acc = None
    for b0 in range(0, blocks * LANES, step):
        g_ref[...] = lax.dot_general(
            a_all, h_ref[:, b0 : b0 + step], (((0,), (0,)), ((), ())), preferred_element_type=f32
        )
        for o in range(0, step, LANES):
            sh = per * ((b0 + o) // LANES)
            part = g_ref[sh : sh + q_len, o : o + LANES]
            acc = part if acc is None else acc + part
    acc_ref[...] = acc
    half = -(-filt // per)
    c_ref[...] = jnp.zeros_like(c_ref)
    for r in range(filt):
        piece = acc_ref[r * ew : r * ew + filt, 0:k]
        for jp in range(1, per):
            piece = piece + acc_ref[r * ew + jp : r * ew + jp + filt, jp * k : (jp + 1) * k]
        at, rr = r // half, r % half
        c_ref[rr * filt : (rr + 1) * filt, at * k : (at + 1) * k] = piece
    hid = jnp.sum(hidden, axis=0, keepdims=True)
    hid = hid + pltpu.roll(hid, LANES // 2, axis=1)
    lane1 = lax.broadcasted_iota(jnp.int32, (1, LANES), 1)
    c_ref[half * filt : half * filt + 1, :] = jnp.where(lane1 < k, hid, jnp.where(lane1 == k, visible, 0.0))

    recv1[me1] = c_ref[...]

    def all_sum(buf, me, size, group, ssem, rsem):
        def copy(d, start):
            other, dev = group(d if start else size - d)
            at = me if start else other
            return pltpu.make_async_remote_copy(
                src_ref=buf.at[me], dst_ref=buf.at[at], send_sem=ssem.at[d], recv_sem=rsem.at[at],
                device_id=dev, device_id_type=MESH,
            )

        for d in range(1, size):
            copy(d, True).start()
        for d in range(1, size):
            copy(d, True).wait_send()
            copy(d, False).wait_recv()
        out = buf[0]
        for i in range(1, size):
            out = out + buf[i]
        return out

    recv2[me2] = all_sum(recv1, me1, n1, group1, s1_sem, r1_sem)
    scale = 1.0 / float(ni * th * tw * n_img * n_row * n_col)
    c_out_ref[...] = all_sum(recv2, me2, n2, group2, s2_sem, r2_sem) * scale


def body(images, filters, hidden_bias, visible_unit_bias, unit_noise):
    ni, th, tw = images.shape
    k, filt, _ = filters.shape
    m = filt // 2
    eh, ew = th + 2 * m, tw + 2 * m
    n_img, n_row, n_col = lax.axis_size("img"), lax.axis_size("row"), lax.axis_size("col")
    rows, wide = ni * th, tw * k
    q = filt * ew
    kp = -(-q // LANES) * LANES
    per = LANES // k
    half = -(-filt // per)
    c_rows = -(-(half * filt + 1) // 8) * 8
    q_len = -(-((filt - 1) * ew + filt + per) // 8) * 8
    top = -(-tw // 16) * 16
    step = 2 * LANES if (wide // LANES) % 2 == 0 else LANES
    fil = jnp.pad(filters.transpose(1, 2, 0), ((0, 0), (0, ew - filt), (0, 0))).reshape(q, k)
    n1, n2 = n_img * n_row, n_col
    vmem = pl.BlockSpec(memory_space=pltpu.VMEM)
    recon, c = pl.pallas_call(
        functools.partial(kernel, (ni, th, tw, k, filt, n_img, n_row, n_col)),
        out_shape=(
            jax.ShapeDtypeStruct((ni, th, tw), bf16),
            jax.ShapeDtypeStruct((c_rows, LANES), f32),
        ),
        in_specs=[vmem, vmem, vmem, pl.BlockSpec(memory_space=pltpu.SMEM), vmem],
        out_specs=(vmem, vmem),
        scratch_shapes=[
            pltpu.VMEM((th, LANES), f32),
            pltpu.VMEM((th, LANES), bf16),
            pltpu.VMEM((9, th, LANES), bf16),
            pltpu.VMEM((eh, LANES), f32),
            pltpu.VMEM((2 * rows, kp), f32),
            pltpu.VMEM((top + kp, LANES), f32),
            pltpu.VMEM((kp, wide), bf16),
            pltpu.VMEM((rows, wide), f32),
            pltpu.VMEM((2 * rows, wide), bf16),
            pltpu.VMEM((rows, wide), bf16),
            pltpu.VMEM((rows, kp), f32),
            pltpu.VMEM((eh, LANES), f32),
            pltpu.VMEM((9, eh, LANES), f32),
            pltpu.VMEM((kp, step), f32),
            pltpu.VMEM((q_len, LANES), f32),
            pltpu.VMEM((c_rows, LANES), f32),
            pltpu.VMEM((n1, c_rows, LANES), f32),
            pltpu.VMEM((n2, c_rows, LANES), f32),
            pltpu.SemaphoreType.DMA((9,)),
            pltpu.SemaphoreType.DMA((9,)),
            pltpu.SemaphoreType.DMA((9,)),
            pltpu.SemaphoreType.DMA((9,)),
            pltpu.SemaphoreType.DMA((n1,)),
            pltpu.SemaphoreType.DMA((n1,)),
            pltpu.SemaphoreType.DMA((n2,)),
            pltpu.SemaphoreType.DMA((n2,)),
        ],
        compiler_params=pltpu.CompilerParams(collective_id=0, has_side_effects=True),
    )(
        images,
        fil,
        hidden_bias.reshape(1, k),
        visible_unit_bias.reshape(1),
        unit_noise.reshape(rows, wide),
    )
    parts = c[: half * filt].reshape(half, filt, per, k)
    grad = parts.transpose(3, 2, 0, 1).reshape(k, per * half, filt)[:, :filt]
    return recon, grad, c[half * filt, :k], c[half * filt, k]


def solution(mesh):
    in_specs = (P("img", "row", "col"), P(), P(), P(), P("img", "row", "col"))
    out_specs = (P("img", "row", "col"), P(), P(), P())
    return jax.shard_map(body, mesh=mesh, in_specs=in_specs, out_specs=out_specs, check_vma=False)
```

profile of v0, /device:TPU:0, one launch (start us, length us, event | category | flops | bytes accessed | tf_op | source)
XLA Modules:
  0.0 32.0 jit_solution(12859353431727819664)
XLA Ops:
  1.3 1.4 %pad.4 = bf16[9,24,64]{2,1,0:T(8,128)(2,1)} pad(bf16[9,9,64]{2,1,0:T(8,128)(2,1)} %bitcast.16, bf16[]{:T(256)} %constant.2.clone.1), padding=0_0x0_15x0_0 | pad | bytes 38018 | tf_op jit(solution)/shard_map/jit(_pad)/pad | solution.py:301
  2.7 24.7 %shard_map.84 = (bf16[4,16,16]{2,1,0:T(8,128)(2,1)}, f32[48,128]{1,0:T(8,128)}) custom-call(bf16[4,16,16]{2,1,0:T(8,128)(2,1)} %img_ref.1, bf16[216,64]{1,0:T(8,128)(2,1)} %bitcast.13, f32[1,64]{1,0:T(1,128)} %bitcast.18, f32[1]{0:T(128)} %bitcast.11.vb_ref, bf16[64,1024]{1,0:T(8,128)(2,1)} %bitcast.15), custom_call_target="tpu_custom_call" | custom-call | tf_op jit(solution)/shard_map/pallas_call | solution.py:304
  27.4 1.3 %slice.15 = f32[1,1]{1,0:T(1,128)} slice(f32[48,128]{1,0:T(8,128)} %get-tuple-element.7), slice={[45:46], [64:65]} | slice | bytes 8 | tf_op jit(solution)/shard_map/slice | solution.py:350
  28.7 1.2 %slice_bitcast_fusion = f32[64]{0:T(128)} fusion(f32[48,128]{1,0:T(8,128)} %get-tuple-element.7), kind=kLoop, calls=%fused_computation | loop fusion | bytes 512 | tf_op jit(solution)/shard_map/squeeze | solution.py:350
  29.9 0.8 %reshape.30 = f32[5,9,2,64]{3,2,1,0:T(2,128)S(1)} reshape(f32[45,128]{1,0:T(8,128)} %bitcast.17) | data formatting | bytes 46080 | tf_op jit(solution)/shard_map/reshape | solution.py:348
  30.7 0.0 copy-start
  30.7 0.6 %slice.16 = f32[64,9,9]{0,2,1:T(8,128)} slice(f32[64,10,9]{0,2,1:T(8,128)S(1)} %bitcast.12), slice={[0:64], [0:9], [0:9]} | slice | bytes 41472 | tf_op jit(solution)/shard_map/slice | solution.py:349
  31.4 0.1 copy-done
  31.4 0.6 %copy.12 = bf16[4,16,16]{2,1,0:T(8,128)(2,1)} copy(bf16[4,16,16]{2,1,0:T(8,128)(2,1)S(1)} %copy-done) | data formatting | bytes 4096
  (1 shorter events, 0.0 us)
Async XLA Ops:
  30.7 0.7 %copy-start = (bf16[4,16,16]{2,1,0:T(8,128)(2,1)S(1)}, bf16[4,16,16]{2,1,0:T(8,128)(2,1)}, u32[]{:S(2)}) copy-start(bf16[4,16,16]{2,1,0:T(8,128)(2,1)} %get-tuple-element.12) | copy-start | bytes 6148
where the time goes:
time: 32.4 us; the launch traced here: 32 us
  Pallas kernels  24.7 us (76%)
  local copies, waits for them, and re-layouts  6.01 us (19%)
  between operations  1.31 us (4%)
    pallas_call x1, Pallas kernels, body(): pl.pallas_call(functools.partial(kernel, (ni, th, tw, k, filt, n_img, n_r...  24.7 us
    pad x1, local copies, waits for them, and re-layouts, body(): jnp.pad(filters.transpose(1, 2, 0), ((0, 0), (0, ew - filt), (0, 0)))  1.41 us
    slice x1, local copies, waits for them, and re-layouts, body(): return (recon, grad, c[half * filt, :k], c[half * filt, k])  1.26 us
    squeeze x1, local copies, waits for them, and re-layouts, body(): return (recon, grad, c[half * filt, :k], c[half * filt, k])  1.19 us
    reshape x1, local copies, waits for them, and re-layouts, body(): parts = c[:half * filt].reshape(half, filt, per, k)  0.83 us
    unnamed x3, local copies, waits for them, and re-layouts  0.68 us

commit v1 on v0

--- a/solution.py
+++ b/solution.py
@@ -28,8 +28,8 @@
 
 
 def kernel(
-    geo, img_ref, fil_ref, hb_ref, vb_ref, noise_ref, recon_ref, c_out_ref,
-    pf, pack, recv_img, ext, a_ref, fp, tz, w_ref, h_ref, s_ref, u_ref, e_ref, recv_e,
+    geo, img_hbm, fil_hbm, hb_hbm, vb_hbm, noise_hbm, recon_hbm, grad_ref, gh_ref, gv_ref,
+    img_ref, fil_ref, hb_ref, vb_ref, noise_ref, recon_ref, in_sem, out_sem, pf, pack, recv_img, ext, a_ref, fp, tz, w_ref, h_ref, s_ref, u_ref, e_ref, recv_e,
     g_ref, acc_ref, c_ref, recv1, recv2, is_sem, ir_sem, es_sem, er_sem, s1_sem, r1_sem, s2_sem, r2_sem,
 ):
     ni, th, tw, k, filt, n_img, n_row, n_col = geo
@@ -63,6 +63,15 @@
         other = lax.rem(me2 + d, n2)
         return other, {"col": other}
 
+    loads = [
+        pltpu.make_async_copy(src, dst, in_sem.at[i])
+        for i, (src, dst) in enumerate(
+            [(img_hbm, img_ref), (fil_hbm, fil_ref), (noise_hbm, noise_ref), (hb_hbm, hb_ref), (vb_hbm, vb_ref)]
+        )
+    ]
+    for load in loads:
+        load.start()
+
     recv_img[...] = jnp.zeros_like(recv_img)
     recv_e[...] = jnp.zeros_like(recv_e)
     barrier = pltpu.get_barrier_semaphore()
@@ -78,28 +87,21 @@
         pl.semaphore_signal(barrier, inc=1, device_id=group2(d)[1], device_id_type=MESH)
 
     pf[...] = jnp.zeros_like(pf)
+    fp[...] = jnp.zeros_like(fp)
+    a_ref[...] = jnp.zeros_like(a_ref)
+    loads[0].wait()
     for n in range(ni):
         pf[:, n * stride + m : n * stride + m + tw] = img_ref[n].astype(f32)
     pack[...] = pf[...].astype(bf16)
 
     top = fp.shape[0] - kp
-    q = fil_ref.shape[0]
-    fp[...] = jnp.zeros_like(fp)
-    fv = fil_ref[...].astype(f32)
     per = LANES // k
-    for jp in range(per):
-        fp[top + jp : top + jp + q, jp * k : (jp + 1) * k] = fv
+    loads[1].wait()
+    for r in range(filt):
+        fv = fil_ref[r].astype(f32)
+        for jp in range(per):
+            fp[top + jp + r * ew : top + jp + r * ew + filt, jp * k : (jp + 1) * k] = fv
     pl.semaphore_wait(barrier, count)
-
-    def exchange(make, start):
-        for d in DIRS:
-            @pl.when(exists(*d))
-            def _(d=d):
-                cp = make(*d)
-                if start:
-                    cp.start()
-                else:
-                    cp.wait()
 
     def img_copy(dr, dc, start):
         at = slot_of(-dr, -dc) if start else slot_of(dr, dc)
@@ -113,10 +115,12 @@
         def _(d=d):
             img_copy(*d, True).start()
 
+    loads[2].wait()
+    loads[3].wait()
+    loads[4].wait()
     for b in range(blocks):
         tz[:, b * LANES : (b + 1) * LANES] = fp[top - per * b : top - per * b + kp, :].astype(bf16)
         w_ref[:, b * LANES : (b + 1) * LANES] = 1.0 / jnp.log(noise_ref[:, b * LANES : (b + 1) * LANES].astype(f32))
-    a_ref[...] = jnp.zeros_like(a_ref)
 
     lane = lax.broadcasted_iota(jnp.int32, (th, LANES), 1) % stride
 
@@ -208,7 +212,7 @@
     total = total + jnp.where(
         jnp.logical_and(elane >= tw, elane < ew), pltpu.roll(right, tw, axis=1), 0.0
     )
-    recon = (total + vb_ref[0]).astype(bf16).astype(f32)
+    recon = (total + vb_ref[...]).astype(bf16).astype(f32)
     lo_r = jnp.where(row_at == 0, m, 0)
     hi_r = jnp.where(row_at == n_row - 1, m + th, eh)
     lo_c = jnp.where(col_at == 0, m, 0)
@@ -218,6 +222,8 @@
     own = ext[m : m + th, :]
     for n in range(ni):
         recon_ref[n] = own[:, n * stride + m : n * stride + m + tw].astype(bf16)
+    out_copy = pltpu.make_async_copy(recon_ref, recon_hbm, out_sem)
+    out_copy.start()
     mine = jnp.logical_and(lane >= m, lane < m + tw)
     visible = jnp.sum(jnp.where(mine, pf[...] - own, 0.0))
     place(rows)
@@ -280,7 +286,14 @@
 
     recv2[me2] = all_sum(recv1, me1, n1, group1, s1_sem, r1_sem)
     scale = 1.0 / float(ni * th * tw * n_img * n_row * n_col)
-    c_out_ref[...] = all_sum(recv2, me2, n2, group2, s2_sem, r2_sem) * scale
+    final = all_sum(recv2, me2, n2, group2, s2_sem, r2_sem) * scale
+    c_ref[...] = final
+    for r in range(filt):
+        at, rr = r // half, r % half
+        grad_ref[r] = c_ref[rr * filt : (rr + 1) * filt, at * k : (at + 1) * k]
+    gh_ref[...] = c_ref[half * filt : half * filt + 1, 0:k]
+    gv_ref[...] = c_ref[half * filt : half * filt + 1, k : k + 1]
+    out_copy.wait()
 
 
 def body(images, filters, hidden_bias, visible_unit_bias, unit_noise):
@@ -298,18 +311,28 @@
     q_len = -(-((filt - 1) * ew + filt + per) // 8) * 8
     top = -(-tw // 16) * 16
     step = 2 * LANES if (wide // LANES) % 2 == 0 else LANES
-    fil = jnp.pad(filters.transpose(1, 2, 0), ((0, 0), (0, ew - filt), (0, 0))).reshape(q, k)
     n1, n2 = n_img * n_row, n_col
     vmem = pl.BlockSpec(memory_space=pltpu.VMEM)
-    recon, c = pl.pallas_call(
+    hbm = pl.BlockSpec(memory_space=pl.ANY)
+    recon, grad, grad_hidden, grad_visible = pl.pallas_call(
         functools.partial(kernel, (ni, th, tw, k, filt, n_img, n_row, n_col)),
         out_shape=(
             jax.ShapeDtypeStruct((ni, th, tw), bf16),
-            jax.ShapeDtypeStruct((c_rows, LANES), f32),
+            jax.ShapeDtypeStruct((filt, filt, k), f32),
+            jax.ShapeDtypeStruct((1, k), f32),
+            jax.ShapeDtypeStruct((1, 1), f32),
         ),
-        in_specs=[vmem, vmem, vmem, pl.BlockSpec(memory_space=pltpu.SMEM), vmem],
-        out_specs=(vmem, vmem),
+        in_specs=[hbm] * 5,
+        out_specs=(hbm, vmem, vmem, vmem),
         scratch_shapes=[
+            pltpu.VMEM((ni, th, tw), bf16),
+            pltpu.VMEM((filt, filt, k), bf16),
+            pltpu.VMEM((1, k), f32),
+            pltpu.VMEM((1, 1), f32),
+            pltpu.VMEM((rows, wide), bf16),
+            pltpu.VMEM((ni, th, tw), bf16),
+            pltpu.SemaphoreType.DMA((5,)),
+            pltpu.SemaphoreType.DMA,
             pltpu.VMEM((th, LANES), f32),
             pltpu.VMEM((th, LANES), bf16),
             pltpu.VMEM((9, th, LANES), bf16),
@@ -340,14 +363,12 @@
         compiler_params=pltpu.CompilerParams(collective_id=0, has_side_effects=True),
     )(
         images,
-        fil,
+        filters.transpose(1, 2, 0),
         hidden_bias.reshape(1, k),
-        visible_unit_bias.reshape(1),
+        visible_unit_bias.reshape(1, 1),
         unit_noise.reshape(rows, wide),
     )
-    parts = c[: half * filt].reshape(half, filt, per, k)
-    grad = parts.transpose(3, 2, 0, 1).reshape(k, per * half, filt)[:, :filt]
-    return recon, grad, c[half * filt, :k], c[half * filt, k]
+    return recon, grad.transpose(2, 0, 1), grad_hidden.reshape(k), grad_visible.reshape(())
 
 
 def solution(mesh):

time: 32.4 us -> 30.8 us (0.951)
  local copies, waits for them, and re-layouts: 6.01 us -> 3.36 us
  between operations: 1.31 us -> 3.1 us
  Pallas kernels: 24.7 us -> 24 us
    unnamed x3 -> x5, local copies, waits for them, and re-layouts: 0.68 us -> 3.36 us
    slice x2 -> x0, local copies, waits for them, and re-layouts: 1.9 us -> none  [the longest x1 1.26 us: body(): return (recon, grad, c[half * filt, :k], c[half * filt, k])]
    pad x1 -> x0, local copies, waits for them, and re-layouts: 1.41 us -> none  [body(): jnp.pad(filters.transpose(1, 2, 0), ((0, 0), (0, ew - filt), (0, 0)))]
    squeeze x1 -> x0, local copies, waits for them, and re-layouts: 1.19 us -> none  [body(): return (recon, grad, c[half * filt, :k], c[half * filt, k])]
    reshape x1 -> x0, local copies, waits for them, and re-layouts: 0.83 us -> none  [body(): parts = c[:half * filt].reshape(half, filt, per, k)]
    pallas_call x1, Pallas kernels: 24.7 us -> 24 us  [body(): pl.pallas_call(functools.partial(kernel, (ni, th, tw, k, filt, n_img, n_r...]
where the time goes in v1:
time: 30.8 us; the launch traced here: 30.4 us
  Pallas kernels  24 us (78%)
  local copies, waits for them, and re-layouts  3.36 us (11%)
  between operations  3.1 us (10%)
    pallas_call x1, Pallas kernels, body(): pl.pallas_call(functools.partial(kernel, (ni, th, tw, k, filt, n_img, n_r...  24 us
    unnamed x5, local copies, waits for them, and re-layouts  3.36 us

profile of v1, /device:TPU:0, one launch (start us, length us, event | category | flops | bytes accessed | tf_op | source)
XLA Modules:
  0.0 30.4 jit_solution(9570648649978097065)
XLA Ops:
  1.3 24.0 %shard_map.84 = (bf16[4,16,16]{2,1,0:T(8,128)(2,1)}, f32[9,9,64]{2,1,0:T(8,128)}, f32[1,64]{1,0:T(1,128)}, f32[1,1]{1,0:T(1,128)}) custom-call(bf16[4,16,16]{2,1,0:T(8,128)(2,1)} %img_hbm.1, bf16[9,9,64]{2,1,0:T(8,128)(2,1)} %bitcast.10, f32[1,64]{1,0:T(1,128)} %bitcast.11, f32[1,1]{1,0:T(1,128)} %bitcast.7.vb_hbm, bf16[64,1024]{1,0:T(8,128)(2,1)} %bitcast.8), custom_call_target="tpu_custom_call" | custom-call | tf_op jit(solution)/shard_map/pallas_call | solution.py:317
  25.2 1.3 %copy.14 = bf16[4,16,16]{2,1,0:T(8,128)(2,1)} copy(bf16[4,16,16]{2,1,0:T(8,128)(2,1)} %get-tuple-element.16) | data formatting | bytes 4096
  26.6 0.0 copy-start
  26.6 1.5 %copy.15 = f32[64,9,9]{0,2,1:T(8,128)} copy(f32[64,9,9]{0,2,1:T(8,128)} %bitcast.9) | data formatting | bytes 41472
  28.1 0.0 copy-done
  28.1 0.5 %copy.16 = f32[64]{0:T(128)} copy(f32[64]{0:T(128)S(1)} %bitcast.12) | data formatting | bytes 512
Async XLA Ops:
  26.6 1.5 %copy-start = (f32[1,64]{1,0:T(1,128)S(1)}, f32[1,64]{1,0:T(1,128)}, u32[]{:S(2)}) copy-start(f32[1,64]{1,0:T(1,128)} %get-tuple-element.10) | copy-start | bytes 772

commit v2 on v1

--- a/solution.py
+++ b/solution.py
@@ -28,7 +28,7 @@
 
 
 def kernel(
-    geo, img_hbm, fil_hbm, hb_hbm, vb_hbm, noise_hbm, recon_hbm, grad_ref, gh_ref, gv_ref,
+    geo, img_hbm, fil_hbm, hb_hbm, vb_hbm, noise_hbm, recon_hbm, c_out_ref,
     img_ref, fil_ref, hb_ref, vb_ref, noise_ref, recon_ref, in_sem, out_sem, pf, pack, recv_img, ext, a_ref, fp, tz, w_ref, h_ref, s_ref, u_ref, e_ref, recv_e,
     g_ref, acc_ref, c_ref, recv1, recv2, is_sem, ir_sem, es_sem, er_sem, s1_sem, r1_sem, s2_sem, r2_sem,
 ):
@@ -286,14 +286,19 @@
 
     recv2[me2] = all_sum(recv1, me1, n1, group1, s1_sem, r1_sem)
     scale = 1.0 / float(ni * th * tw * n_img * n_row * n_col)
-    final = all_sum(recv2, me2, n2, group2, s2_sem, r2_sem) * scale
-    c_ref[...] = final
+    c_out_ref[...] = all_sum(recv2, me2, n2, group2, s2_sem, r2_sem) * scale
+    out_copy.wait()
+
+
+def unpack(geo, recon_in, c_ref, recon_ref, grad_ref, gh_ref, gv_ref):
+    filt, k = geo
+    half = -(-filt // (LANES // k))
+    recon_ref[...] = recon_in[...]
     for r in range(filt):
         at, rr = r // half, r % half
         grad_ref[r] = c_ref[rr * filt : (rr + 1) * filt, at * k : (at + 1) * k]
     gh_ref[...] = c_ref[half * filt : half * filt + 1, 0:k]
     gv_ref[...] = c_ref[half * filt : half * filt + 1, k : k + 1]
-    out_copy.wait()
 
 
 def body(images, filters, hidden_bias, visible_unit_bias, unit_noise):
@@ -314,16 +319,14 @@
     n1, n2 = n_img * n_row, n_col
     vmem = pl.BlockSpec(memory_space=pltpu.VMEM)
     hbm = pl.BlockSpec(memory_space=pl.ANY)
-    recon, grad, grad_hidden, grad_visible = pl.pallas_call(
+    recon, c = pl.pallas_call(
         functools.partial(kernel, (ni, th, tw, k, filt, n_img, n_row, n_col)),
         out_shape=(
             jax.ShapeDtypeStruct((ni, th, tw), bf16),
-            jax.ShapeDtypeStruct((filt, filt, k), f32),
-            jax.ShapeDtypeStruct((1, k), f32),
-            jax.ShapeDtypeStruct((1, 1), f32),
+            jax.ShapeDtypeStruct((c_rows, LANES), f32),
         ),
         in_specs=[hbm] * 5,
-        out_specs=(hbm, vmem, vmem, vmem),
+        out_specs=(hbm, vmem),
         scratch_shapes=[
             pltpu.VMEM((ni, th, tw), bf16),
             pltpu.VMEM((filt, filt, k), bf16),
@@ -368,6 +371,17 @@
         visible_unit_bias.reshape(1, 1),
         unit_noise.reshape(rows, wide),
     )
+    recon, grad, grad_hidden, grad_visible = pl.pallas_call(
+        functools.partial(unpack, (filt, k)),
+        out_shape=(
+            jax.ShapeDtypeStruct((ni, th, tw), bf16),
+            jax.ShapeDtypeStruct((filt, filt, k), f32),
+            jax.ShapeDtypeStruct((1, k), f32),
+            jax.ShapeDtypeStruct((1, 1), f32),
+        ),
+        in_specs=[vmem, vmem],
+        out_specs=(vmem,) * 4,
+    )(recon, c)
     return recon, grad.transpose(2, 0, 1), grad_hidden.reshape(k), grad_visible.reshape(())
 
 

time: 30.8 us -> 26.9 us (0.87)
  local copies, waits for them, and re-layouts: 3.36 us -> 0 us
  between operations: 3.1 us -> 1.29 us
  Pallas kernels: 24 us -> 25.3 us
    unnamed x5 -> x0, local copies, waits for them, and re-layouts: 3.36 us -> none
    pallas_call x0 -> x1, Pallas kernels: none -> 1.47 us  [body(): pl.pallas_call(functools.partial(unpack, (filt, k)), out_shape=(jax.Shape...]
where the time goes in v2:
time: 26.9 us; the launch traced here: 26.6 us
  Pallas kernels  25.3 us (94%)
  between operations  1.29 us (5%)
    pallas_call x1, Pallas kernels, body(): pl.pallas_call(functools.partial(kernel, (ni, th, tw, k, filt, n_img, n_r...  23.9 us
    pallas_call x1, Pallas kernels, body(): pl.pallas_call(functools.partial(unpack, (filt, k)), out_shape=(jax.Shape...  1.47 us

profile of v2, /device:TPU:0, one launch (start us, length us, event | category | flops | bytes accessed | tf_op | source)
XLA Modules:
  0.0 26.6 jit_solution(1728313502026328478)
XLA Ops:
  1.3 23.9 %shard_map.84 = (bf16[4,16,16]{2,1,0:T(8,128)(2,1)}, f32[48,128]{1,0:T(8,128)}) custom-call(bf16[4,16,16]{2,1,0:T(8,128)(2,1)} %img_hbm.1, bf16[9,9,64]{2,1,0:T(8,128)(2,1)} %bitcast.9, f32[1,64]{1,0:T(1,128)} %bitcast.10, f32[1,1]{1,0:T(1,128)} %bitcast.7.vb_hbm, bf16[64,1024]{1,0:T(8,128)(2,1)} %bitcast.8), custom_call_target="tpu_custom_call" | custom-call | tf_op jit(solution)/shard_map/pallas_call | solution.py:322
  25.1 1.5 %shard_map.85 = (bf16[4,16,16]{2,1,0:T(8,128)(2,1)}, f32[9,9,64]{2,1,0:T(8,128)}, f32[1,64]{1,0:T(1,128)}, f32[1,1]{1,0:T(1,128)}) custom-call(bf16[4,16,16]{2,1,0:T(8,128)(2,1)} %get-tuple-element.10.recon_in, f32[48,128]{1,0:T(8,128)} %get-tuple-element.11.c_ref), custom_call_target="tpu_custom_call" | custom-call | tf_op jit(solution)/shard_map/pallas_call | solution.py:374

commit v3 on v2

--- a/solution.py
+++ b/solution.py
@@ -28,8 +28,8 @@
 
 
 def kernel(
-    geo, img_hbm, fil_hbm, hb_hbm, vb_hbm, noise_hbm, recon_hbm, c_out_ref,
-    img_ref, fil_ref, hb_ref, vb_ref, noise_ref, recon_ref, in_sem, out_sem, pf, pack, recv_img, ext, a_ref, fp, tz, w_ref, h_ref, s_ref, u_ref, e_ref, recv_e,
+    geo, img_hbm, fil_hbm, hb_hbm, vb_hbm, noise_hbm, recon_ref, c_out_ref,
+    img_ref, fil_ref, hb_ref, vb_ref, noise_ref, in_sem, pf, pack, recv_img, ext, a_ref, fp, tz, w_ref, h_ref, s_ref, u_ref, e_ref, recv_e,
     g_ref, acc_ref, c_ref, recv1, recv2, is_sem, ir_sem, es_sem, er_sem, s1_sem, r1_sem, s2_sem, r2_sem,
 ):
     ni, th, tw, k, filt, n_img, n_row, n_col = geo
@@ -222,8 +222,6 @@
     own = ext[m : m + th, :]
     for n in range(ni):
         recon_ref[n] = own[:, n * stride + m : n * stride + m + tw].astype(bf16)
-    out_copy = pltpu.make_async_copy(recon_ref, recon_hbm, out_sem)
-    out_copy.start()
     mine = jnp.logical_and(lane >= m, lane < m + tw)
     visible = jnp.sum(jnp.where(mine, pf[...] - own, 0.0))
     place(rows)
@@ -287,7 +285,6 @@
     recv2[me2] = all_sum(recv1, me1, n1, group1, s1_sem, r1_sem)
     scale = 1.0 / float(ni * th * tw * n_img * n_row * n_col)
     c_out_ref[...] = all_sum(recv2, me2, n2, group2, s2_sem, r2_sem) * scale
-    out_copy.wait()
 
 
 def unpack(geo, recon_in, c_ref, recon_ref, grad_ref, gh_ref, gv_ref):
@@ -322,20 +319,18 @@
     recon, c = pl.pallas_call(
         functools.partial(kernel, (ni, th, tw, k, filt, n_img, n_row, n_col)),
         out_shape=(
-            jax.ShapeDtypeStruct((ni, th, tw), bf16),
-            jax.ShapeDtypeStruct((c_rows, LANES), f32),
+            pltpu.VMEM((ni, th, tw), bf16),
+            pltpu.VMEM((c_rows, LANES), f32),
         ),
         in_specs=[hbm] * 5,
-        out_specs=(hbm, vmem),
+        out_specs=(vmem, vmem),
         scratch_shapes=[
             pltpu.VMEM((ni, th, tw), bf16),
             pltpu.VMEM((filt, filt, k), bf16),
             pltpu.VMEM((1, k), f32),
             pltpu.VMEM((1, 1), f32),
             pltpu.VMEM((rows, wide), bf16),
-            pltpu.VMEM((ni, th, tw), bf16),
             pltpu.SemaphoreType.DMA((5,)),
-            pltpu.SemaphoreType.DMA,
             pltpu.VMEM((th, LANES), f32),
             pltpu.VMEM((th, LANES), bf16),
             pltpu.VMEM((9, th, LANES), bf16),
@@ -381,7 +376,7 @@
         ),
         in_specs=[vmem, vmem],
         out_specs=(vmem,) * 4,
-    )(recon, c)
+    )(*[pltpu.with_memory_space_constraint(x, pltpu.VMEM) for x in (recon, c)])
     return recon, grad.transpose(2, 0, 1), grad_hidden.reshape(k), grad_visible.reshape(())
 
 

time: 26.9 us -> 25.5 us (0.948)
  Pallas kernels: 25.3 us -> 24 us
    pallas_call x1, Pallas kernels: 1.47 us -> 0.71 us  [body(): pl.pallas_call(functools.partial(unpack, (filt, k)), out_shape=(jax.Shape...]
    pallas_call x1, Pallas kernels: 23.9 us -> 23.2 us  [body(): pl.pallas_call(functools.partial(kernel, (ni, th, tw, k, filt, n_img, n_r...]
where the time goes in v3:
time: 25.5 us; the launch traced here: 25.2 us
  Pallas kernels  24 us (94%)
  between operations  1.29 us (5%)
    pallas_call x1, Pallas kernels, body(): pl.pallas_call(functools.partial(kernel, (ni, th, tw, k, filt, n_img, n_r...  23.2 us
    pallas_call x1, Pallas kernels, body(): pl.pallas_call(functools.partial(unpack, (filt, k)), out_shape=(jax.Shape...  0.71 us

profile of v3, /device:TPU:0, one launch (start us, length us, event | category | flops | bytes accessed | tf_op | source)
XLA Modules:
  0.0 25.2 jit_solution(17509217810794218813)
XLA Ops:
  1.3 23.2 %shard_map.84 = (bf16[4,16,16]{2,1,0:T(8,128)(2,1)S(1)}, f32[48,128]{1,0:T(8,128)S(1)}) custom-call(bf16[4,16,16]{2,1,0:T(8,128)(2,1)} %img_hbm.1, bf16[9,9,64]{2,1,0:T(8,128)(2,1)} %bitcast.9, f32[1,64]{1,0:T(1,128)} %bitcast.10, f32[1,1]{1,0:T(1,128)} %bitcast.7.vb_hbm, bf16[64,1024]{1,0:T(8,128)(2,1)} %bitcast.8), custom_call_target="tpu_custom_call" | custom-call | tf_op jit(solution)/shard_map/pallas_call | solution.py:319
  24.5 0.7 %shard_map.85 = (bf16[4,16,16]{2,1,0:T(8,128)(2,1)}, f32[9,9,64]{2,1,0:T(8,128)}, f32[1,64]{1,0:T(1,128)}, f32[1,1]{1,0:T(1,128)}) custom-call(bf16[4,16,16]{2,1,0:T(8,128)(2,1)S(1)} %get-tuple-element.10.recon_in, f32[48,128]{1,0:T(8,128)S(1)} %get-tuple-element.11.c_ref), custom_call_target="tpu_custom_call" | custom-call | tf_op jit(solution)/shard_map/pallas_call | solution.py:369

commit v4 on v3

--- a/solution.py
+++ b/solution.py
@@ -30,7 +30,7 @@
 def kernel(
     geo, img_hbm, fil_hbm, hb_hbm, vb_hbm, noise_hbm, recon_ref, c_out_ref,
     img_ref, fil_ref, hb_ref, vb_ref, noise_ref, in_sem, pf, pack, recv_img, ext, a_ref, fp, tz, w_ref, h_ref, s_ref, u_ref, e_ref, recv_e,
-    g_ref, acc_ref, c_ref, recv1, recv2, is_sem, ir_sem, es_sem, er_sem, s1_sem, r1_sem, s2_sem, r2_sem,
+    g_ref, acc_ref, call_ref, c_ref, recv1, recv2, recv3, is_sem, ir_sem, es_sem, er_sem, s1_sem, r1_sem, s2_sem, r2_sem, s3_sem, r3_sem,
 ):
     ni, th, tw, k, filt, n_img, n_row, n_col = geo
     m = filt // 2
@@ -249,42 +249,75 @@
             acc = part if acc is None else acc + part
     acc_ref[...] = acc
     half = -(-filt // per)
-    c_ref[...] = jnp.zeros_like(c_ref)
+    call_ref[...] = jnp.zeros_like(call_ref)
     for r in range(filt):
         piece = acc_ref[r * ew : r * ew + filt, 0:k]
         for jp in range(1, per):
             piece = piece + acc_ref[r * ew + jp : r * ew + jp + filt, jp * k : (jp + 1) * k]
         at, rr = r // half, r % half
-        c_ref[rr * filt : (rr + 1) * filt, at * k : (at + 1) * k] = piece
+        call_ref[rr * filt : (rr + 1) * filt, at * k : (at + 1) * k] = piece
     hid = jnp.sum(hidden, axis=0, keepdims=True)
     hid = hid + pltpu.roll(hid, LANES // 2, axis=1)
     lane1 = lax.broadcasted_iota(jnp.int32, (1, LANES), 1)
-    c_ref[half * filt : half * filt + 1, :] = jnp.where(lane1 < k, hid, jnp.where(lane1 == k, visible, 0.0))
-
-    recv1[me1] = c_ref[...]
-
-    def all_sum(buf, me, size, group, ssem, rsem):
-        def copy(d, start):
-            other, dev = group(d if start else size - d)
-            at = me if start else other
-            return pltpu.make_async_remote_copy(
-                src_ref=buf.at[me], dst_ref=buf.at[at], send_sem=ssem.at[d], recv_sem=rsem.at[at],
-                device_id=dev, device_id_type=MESH,
-            )
-
-        for d in range(1, size):
-            copy(d, True).start()
-        for d in range(1, size):
-            copy(d, True).wait_send()
-            copy(d, False).wait_recv()
-        out = buf[0]
-        for i in range(1, size):
-            out = out + buf[i]
-        return out
-
-    recv2[me2] = all_sum(recv1, me1, n1, group1, s1_sem, r1_sem)
+    call_ref[half * filt : half * filt + 1, :] = jnp.where(lane1 < k, hid, jnp.where(lane1 == k, visible, 0.0))
+    for i in range(n_img):
+        c_ref[i] = call_ref[i * c_ref.shape[1] : (i + 1) * c_ref.shape[1], :]
+
+    deep = recv1.shape[1]
+
+    def give1(d):
+        other, dev = group1(d)
+        return other, dev, lax.div(other, n_row)
+
+    def send(src, dst, ssem, rsem, dev):
+        return pltpu.make_async_remote_copy(
+            src_ref=src, dst_ref=dst, send_sem=ssem, recv_sem=rsem, device_id=dev, device_id_type=MESH
+        )
+
+    for d in range(1, n1):
+        other, dev, part = give1(d)
+        send(c_ref.at[part], recv1.at[me1], s1_sem.at[d], r1_sem.at[me1], dev).start()
+    recv1[me1] = c_ref[img_at]
+    for d in range(1, n1):
+        other, dev, part = give1(d)
+        send(c_ref.at[part], recv1.at[other], s1_sem.at[d], r1_sem.at[other], dev).wait_recv()
+    out = recv1[0]
+    for i in range(1, n1):
+        out = out + recv1[i]
+    recv2[me2] = out
+    for d in range(1, n2):
+        other, dev = group2(d)
+        send(recv2.at[me2], recv2.at[me2], s2_sem.at[d], r2_sem.at[me2], dev).start()
+    for d in range(1, n2):
+        other, dev = group2(d)
+        send(recv2.at[me2], recv2.at[other], s2_sem.at[d], r2_sem.at[other], dev).wait_recv()
+    out = recv2[0]
+    for i in range(1, n2):
+        out = out + recv2[i]
     scale = 1.0 / float(ni * th * tw * n_img * n_row * n_col)
-    c_out_ref[...] = all_sum(recv2, me2, n2, group2, s2_sem, r2_sem) * scale
+    recv3[img_at] = out * scale
+
+    def group3(d):
+        other = lax.rem(img_at + d, n_img)
+        return other, {"img": other}
+
+    for d in range(1, n_img):
+        other, dev = group3(d)
+        send(recv3.at[img_at], recv3.at[img_at], s3_sem.at[d], r3_sem.at[img_at], dev).start()
+    for d in range(1, n_img):
+        other, dev = group3(d)
+        send(recv3.at[img_at], recv3.at[other], s3_sem.at[d], r3_sem.at[other], dev).wait_recv()
+    for i in range(n_img):
+        c_out_ref[i * deep : (i + 1) * deep, :] = recv3[i]
+    for d in range(1, n1):
+        other, dev, part = give1(d)
+        send(c_ref.at[part], recv1.at[me1], s1_sem.at[d], r1_sem.at[me1], dev).wait_send()
+    for d in range(1, n2):
+        other, dev = group2(d)
+        send(recv2.at[me2], recv2.at[me2], s2_sem.at[d], r2_sem.at[me2], dev).wait_send()
+    for d in range(1, n_img):
+        other, dev = group3(d)
+        send(recv3.at[img_at], recv3.at[img_at], s3_sem.at[d], r3_sem.at[img_at], dev).wait_send()
 
 
 def unpack(geo, recon_in, c_ref, recon_ref, grad_ref, gh_ref, gv_ref):
@@ -309,7 +342,7 @@
     kp = -(-q // LANES) * LANES
     per = LANES // k
     half = -(-filt // per)
-    c_rows = -(-(half * filt + 1) // 8) * 8
+    c_rows = -(-(half * filt + 1) // (8 * n_img)) * 8 * n_img
     q_len = -(-((filt - 1) * ew + filt + per) // 8) * 8
     top = -(-tw // 16) * 16
     step = 2 * LANES if (wide // LANES) % 2 == 0 else LANES
@@ -347,8 +380,10 @@
             pltpu.VMEM((kp, step), f32),
             pltpu.VMEM((q_len, LANES), f32),
             pltpu.VMEM((c_rows, LANES), f32),
-            pltpu.VMEM((n1, c_rows, LANES), f32),
-            pltpu.VMEM((n2, c_rows, LANES), f32),
+            pltpu.VMEM((n_img, c_rows // n_img, LANES), f32),
+            pltpu.VMEM((n1, c_rows // n_img, LANES), f32),
+            pltpu.VMEM((n2, c_rows // n_img, LANES), f32),
+            pltpu.VMEM((n_img, c_rows // n_img, LANES), f32),
             pltpu.SemaphoreType.DMA((9,)),
             pltpu.SemaphoreType.DMA((9,)),
             pltpu.SemaphoreType.DMA((9,)),
@@ -357,6 +392,8 @@
             pltpu.SemaphoreType.DMA((n1,)),
             pltpu.SemaphoreType.DMA((n2,)),
             pltpu.SemaphoreType.DMA((n2,)),
+            pltpu.SemaphoreType.DMA((n_img,)),
+            pltpu.SemaphoreType.DMA((n_img,)),
         ],
         compiler_params=pltpu.CompilerParams(collective_id=0, has_side_effects=True),
     )(

time: 25.5 us -> 25.2 us (0.988)
  Pallas kernels: 24 us -> 23.6 us
    pallas_call x1, Pallas kernels: 23.2 us -> 22.9 us  [body(): pl.pallas_call(functools.partial(kernel, (ni, th, tw, k, filt, n_img, n_r...]
where the time goes in v4:
time: 25.2 us; the launch traced here: 24.9 us
  Pallas kernels  23.6 us (94%)
  between operations  1.29 us (5%)
    pallas_call x1, Pallas kernels, body(): pl.pallas_call(functools.partial(kernel, (ni, th, tw, k, filt, n_img, n_r...  22.9 us
    pallas_call x1, Pallas kernels, body(): pl.pallas_call(functools.partial(unpack, (filt, k)), out_shape=(jax.Shape...  0.71 us

profile of v4, /device:TPU:0, one launch (start us, length us, event | category | flops | bytes accessed | tf_op | source)
XLA Modules:
  0.0 24.9 jit_solution(17783931875316950797)
XLA Ops:
  1.3 22.9 %shard_map.84 = (bf16[4,16,16]{2,1,0:T(8,128)(2,1)S(1)}, f32[48,128]{1,0:T(8,128)S(1)}) custom-call(bf16[4,16,16]{2,1,0:T(8,128)(2,1)} %img_hbm.1, bf16[9,9,64]{2,1,0:T(8,128)(2,1)} %bitcast.9, f32[1,64]{1,0:T(1,128)} %bitcast.10, f32[1,1]{1,0:T(1,128)} %bitcast.7.vb_hbm, bf16[64,1024]{1,0:T(8,128)(2,1)} %bitcast.8), custom_call_target="tpu_custom_call" | custom-call | tf_op jit(solution)/shard_map/pallas_call | solution.py:352
  24.2 0.7 %shard_map.85 = (bf16[4,16,16]{2,1,0:T(8,128)(2,1)}, f32[9,9,64]{2,1,0:T(8,128)}, f32[1,64]{1,0:T(1,128)}, f32[1,1]{1,0:T(1,128)}) custom-call(bf16[4,16,16]{2,1,0:T(8,128)(2,1)S(1)} %get-tuple-element.10.recon_in, f32[48,128]{1,0:T(8,128)S(1)} %get-tuple-element.11.c_ref), custom_call_target="tpu_custom_call" | custom-call | tf_op jit(solution)/shard_map/pallas_call | solution.py:406
